TPU v7x, 32 devices: a whole 2x2x4 slice. The times are simulated.
32 devices in a mesh: groups: 2 (over y), rows: 4 (over z), cols: 4 (over x, core).
Axes of the slice: x: 2, y: 2, z: 4, core: 2. Of those that a mesh axis runs over, the one named last changes fastest.
Arguments:
- hidden: bfloat16 [64, 32, 1280], P(('groups', 'rows'), 'cols'), parts along dimension 0, may hold values from -6 to 6
- ln_gain: float32 [1280], replicated, may hold values from 0.1 to 1.9
- ln_bias: float32 [1280], replicated, may hold values from -3 to 3
- w_query: bfloat16 [1280, 256], P(None, 'cols'), may hold values from -8.944272 to 8.944272
- w_keyval: bfloat16 [1280, 512], P(None, 'cols'), may hold values from -0.3125 to 0.3125
- stale_keyval: bfloat16 [64, 32, 4, 128], P(('groups', 'rows'), None, 'cols'), parts along dimension 0, may hold values from -10 to 10
- w_out: bfloat16 [256, 1280], replicated, may hold values from -0.375 to 0.375
- out_bias: float32 [1280], replicated, may hold values from -3 to 3
Outputs:
- output_rows: bfloat16 [64, 32, 1280], P(('groups', 'rows'), 'cols'), parts along dimension 0
- fresh_keyval: bfloat16 [64, 32, 4, 128], P(('groups', 'rows'), None, 'cols'), parts along dimension 0
There are 2 independent parts, one for each index of `groups`. A program takes and returns all parts, laid end to end along the dimension named above; an argument that names none is the same for every part. Nothing has to cross between parts.
All inputs are finite; a program needn't handle non-finite values.
Results may differ from a plain program's by a relative error of at most 0.04.
The roundings to bfloat16 on the way count: a program that leaves them out, or rounds other values in their place, can miss the bound.
Values may be sent and summed in bfloat16 or wider, within the bound.
No kernel may reach another device: no remote copies, remote signals or barrier semaphores. Data moves between devices by JAX's collectives and lax.ppermute only.
A program may use at most 64 MiB of HBM per device.

v0:
```python
import math
import jax
import jax.numpy as jnp
from jax import lax
from jax.sharding import PartitionSpec as P


def layer_norm(hidden, ln_gain, ln_bias):
    values = hidden.astype(jnp.float32)
    row_mean = jnp.mean(values, axis=-1, keepdims=True)
    centred = values - row_mean
    variance = jnp.mean(centred * centred, axis=-1, keepdims=True)
    return (centred * lax.rsqrt(variance + 1e-05) * ln_gain + ln_bias).astype(jnp.bfloat16)


def absorb(running, key_block, queries, score_scale):
    row_max, denominator, weighted = running
    head_size = queries.shape[1]
    scores = (
        jnp.dot(queries, key_block[:, :head_size].T, preferred_element_type=jnp.float32)
        * score_scale
    )
    new_max = jnp.maximum(row_max, jnp.max(scores, axis=-1))
    factor = jnp.exp(row_max - new_max)
    probability = jnp.exp(scores - new_max[:, None])
    denominator = denominator * factor + jnp.sum(probability, axis=-1)
    weighted = weighted * factor[:, None] + jnp.dot(
        probability.astype(jnp.bfloat16),
        key_block[:, head_size:],
        preferred_element_type=jnp.float32,
    )
    return (new_max, denominator, weighted)


def shards(hidden, ln_gain, ln_bias, w_query, w_keyval, stale_keyval, w_out, out_bias):
    band_rows, strip_cols, channels = hidden.shape
    head_size = w_query.shape[1]
    normed = layer_norm(hidden, ln_gain, ln_bias)
    both_weights = jnp.concatenate([w_query, w_keyval], axis=1)
    projected = jnp.dot(
        lax.all_gather(normed, "cols", axis=1, tiled=True),
        both_weights,
        preferred_element_type=jnp.float32,
    ).astype(jnp.bfloat16)
    full_cols = projected.shape[1]
    queries = projected[:, :, :head_size].reshape(-1, head_size)
    keyval = projected[:, :, head_size:]
    fresh_flat = keyval.reshape(-1, 2 * head_size)
    own_band = lax.axis_index("rows")
    score_scale = 1.0 / math.sqrt(head_size)
    query_count = queries.shape[0]
    initial = (
        jnp.full((query_count,), -1e30, jnp.float32),
        jnp.zeros((query_count,), jnp.float32),
        jnp.zeros((query_count, head_size), jnp.float32),
    )
    received = lax.all_gather(stale_keyval, "rows", axis=0, tiled=True)
    band_count = received.shape[0] // band_rows
    key_blocks = received.reshape(band_count, band_rows * full_cols, 2 * head_size)

    def step_band(state, position):
        key_block = jnp.where(position == own_band, fresh_flat, key_blocks[position])
        return (absorb(state, key_block, queries, score_scale), None)

    folded, unused = lax.scan(step_band, initial, jnp.arange(band_count, dtype=jnp.int32))
    row_max, denominator, weighted = folded
    attention = (
        (weighted / denominator[:, None])
        .astype(jnp.bfloat16)
        .reshape(band_rows, full_cols, 1, head_size)
    )
    values = lax.all_to_all(attention, "cols", split_axis=1, concat_axis=2, tiled=True)
    row_count = values.shape[0]
    flat_values = values.reshape(row_count * values.shape[1], values.shape[2] * values.shape[3])
    result = jnp.dot(flat_values, w_out, preferred_element_type=jnp.float32)
    projected_out = result.reshape(row_count, values.shape[1], channels)
    output_rows = (projected_out + out_bias + hidden.astype(jnp.float32)).astype(jnp.bfloat16)
    return (output_rows, keyval.reshape(band_rows, full_cols, 1, 2 * head_size))


def solution(mesh):
    return jax.shard_map(
        shards,
        mesh=mesh,
        in_specs=(
            P(("groups", "rows"), "cols", None),
            P(),
            P(),
            P(None, "cols"),
            P(None, "cols"),
            P(("groups", "rows"), None, "cols", None),
            P(),
            P(),
        ),
        out_specs=(P(("groups", "rows"), "cols", None), P(("groups", "rows"), None, "cols", None)),
        check_vma=False,
    )
```

profile of v0, /device:TPU:0, one launch (start us, length us, event | category | flops | bytes accessed | tf_op | source)
XLA Modules:
  0.0 53.3 jit_solution(13207126210081687228)
XLA Ops:
  0.6 0.0 copy-start
  0.6 0.0 copy-start.1
  0.7 1.1 %convert_reduce_fusion = f32[8,8]{1,0:T(8,128)S(1)} fusion(bf16[8,8,1280]{2,1,0:T(8,128)(2,1)} %param.10), kind=kLoop, calls=%fused_computation.24 | loop fusion | flops 163776 | bytes 164096 | tf_op jit(solution)/shard_map/reduce_sum | solution.py:10
  1.8 0.0 copy-done.1
  1.8 0.0 copy-start.7
  1.8 0.2 fusion.15
  2.0 0.0 copy-start.6
  2.0 0.5 copy-done.7
  2.5 0.2 copy-done.6
  2.7 0.1 fusion.18
  2.8 0.0 copy-start.3
  2.8 9.5 %all_gather.7 = bf16[8,32,1280]{2,1,0:T(8,128)(2,1)S(1)} all-gather(bf16[8,8,1280]{2,1,0:T(8,128)(2,1)S(1)} %fusion.18), channel_id=1, replica_groups=mesh['groups'=2,'rows'=4,'cols'=4] {'cols'}, dimensions={1}, use_global_device_ids=true | all-gather | bytes 819200 | tf_op jit(solution)/shard_map/all_gather | solution.py:41
  12.3 0.0 copy-done.3
  12.3 0.0 copy-start.8
  12.3 0.2 copy.16
  12.5 0.7 %copy-done.8 = bf16[1280,64]{0,1:T(8,128)(2,1)S(1)} copy-done((bf16[1280,64]{0,1:T(8,128)(2,1)S(1)}, bf16[1280,64]{0,1:T(8,128)(2,1)}, u32[]{:S(2)}) %copy-start.8) | copy-done | bytes 163864
  13.2 0.3 convolution_convert_fusion
  13.6 0.0 copy-start.2
  13.6 0.7 %slice_bitcast_fusion = (bf16[8,32,1,128]{3,1,2,0:T(8,128)(2,1)}, bf16[8,32,128]{2,1,0:T(8,128)(2,1)S(1)}) fusion(bf16[8,32,192]{2,1,0:T(8,128)(2,1)S(1)} %convolution_convert_fusion), kind=kLoop, calls=%fused_computation.36 | loop fusion | bytes 196608
  14.3 0.0 copy-done.2
  14.3 0.0 copy-start.4
  14.3 0.8 %copy-done.4 = bf16[8,32,1,128]{3,1,2,0:T(8,128)(2,1)S(1)} copy-done((bf16[8,32,1,128]{3,1,2,0:T(8,128)(2,1)S(1)}, bf16[8,32,1,128]{3,1,2,0:T(8,128)(2,1)}, u32[]{:S(2)}) %copy-start.4) | copy-done | bytes 65560
  15.2 0.0 slice-start
  15.2 14.3 %all_gather.6 = bf16[32,32,1,128]{3,1,2,0:T(8,128)(2,1)S(1)} all-gather(bf16[8,32,1,128]{3,1,2,0:T(8,128)(2,1)S(1)} %copy-done.4), channel_id=1, replica_groups=mesh['groups'=2,'rows'=4,'cols'=4] {'rows'}, dimensions={0}, use_global_device_ids=true | all-gather | bytes 327680 | tf_op jit(solution)/shard_map/all_gather | solution.py:57
  29.5 0.0 slice-done
  29.5 15.4 %while.15 = (s32[]{:T(128)}, f32[256]{0:T(256)S(1)}, f32[256]{0:T(256)S(1)}, f32[256,64]{0,1:T(8,128)S(1)}, s32[4]{0:T(128)S(1)}, /*index=5*/s32[]{:T(128)}, bf1...) while((s32[]{:T(128)}, f32[256]{0:T(256)S(1)}, ...), condition=%wide.region_5.6_spmd.clone, body=%wide.region_2.5_spmd.clone.sunk | while | flops 17253640 | bytes 1294525 | solution.py:65
  29.5 0.6 %dynamic_slice.13 = s32[1]{0:T(128)} dynamic-slice(s32[4]{0:T(128)S(1)} %get-tuple-element.203, s32[]{:T(128)} %get-tuple-element.187), dynamic_slice_sizes={1} | dynamic-slice | bytes 12 | tf_op jit(solution)/shard_map/while/body/jit(dynamic_index_in_dim)/dynamic_slice | solution.py:65
  32.7 0.2 fusion.34
  32.9 0.1 fusion.36
  33.0 0.3 convolution_add_fusion.3
  33.3 0.6 %dynamic_slice.13 = s32[1]{0:T(128)} dynamic-slice(s32[4]{0:T(128)S(1)} %get-tuple-element.203, s32[]{:T(128)} %get-tuple-element.187), dynamic_slice_sizes={1} | dynamic-slice | bytes 12 | tf_op jit(solution)/shard_map/while/body/jit(dynamic_index_in_dim)/dynamic_slice | solution.py:65
  36.5 0.2 fusion.34
  36.8 0.1 fusion.36
  36.9 0.3 convolution_add_fusion.3
  37.2 0.6 %dynamic_slice.13 = s32[1]{0:T(128)} dynamic-slice(s32[4]{0:T(128)S(1)} %get-tuple-element.203, s32[]{:T(128)} %get-tuple-element.187), dynamic_slice_sizes={1} | dynamic-slice | bytes 12 | tf_op jit(solution)/shard_map/while/body/jit(dynamic_index_in_dim)/dynamic_slice | solution.py:65
  40.4 0.2 fusion.34
  40.6 0.1 fusion.36
  40.7 0.3 convolution_add_fusion.3
  41.0 0.6 %dynamic_slice.13 = s32[1]{0:T(128)} dynamic-slice(s32[4]{0:T(128)S(1)} %get-tuple-element.203, s32[]{:T(128)} %get-tuple-element.187), dynamic_slice_sizes={1} | dynamic-slice | bytes 12 | tf_op jit(solution)/shard_map/while/body/jit(dynamic_index_in_dim)/dynamic_slice | solution.py:65
  44.2 0.2 fusion.34
  44.5 0.1 fusion.36
  44.6 0.3 convolution_add_fusion.3
  44.9 0.1 copy.17
  45.0 0.1 divide_convert_fusion
  45.1 0.1 reshape.49
  45.2 6.3 %all_to_all.15 = bf16[4,2,2048]{2,1,0:T(2,128)(2,1)S(1)} all-to-all(bf16[4,2,2048]{2,1,0:T(2,128)(2,1)S(1)} %reshape.49), channel_id=1, replica_groups=mesh['groups'=2,'rows'=4,'cols'=4] {'cols'}, dimensions={0} | all-to-all | bytes 65536 | tf_op jit(solution)/shard_map/all_to_all | solution.py:72
  51.5 0.1 reshape.50
  51.7 0.0 copy-start.5
  51.7 0.1 dot_general.15
  51.8 0.0 copy-done
  51.8 0.6 %copy-done.5 = f32[1280]{0:T(1024)S(1)} copy-done((f32[1280]{0:T(1024)S(1)}, f32[1280]{0:T(1024)}, u32[]{:S(2)}) %copy-start.5) | copy-done | bytes 5144
  52.4 0.9 %fusion.9 = bf16[8,8,1280]{2,1,0:T(8,128)(2,1)} fusion(bf16[8,8,256]{2,1,0:T(8,128)(2,1)S(1)} %dot_general.15, bf16[256,1280]{1,0:T(8,128)(2,1)S(1)} %copy-done, bf16[8,8,1280]{2,1,0:T(8,128)(2,1)S(1)} %copy-done.1, f32[1280]{0:T(1024)S(1)} %copy-done.5), kind=kOutput, calls=%fused_computation.17 | convolution fusion | flops 42270720 | bytes 1020928 | tf_op jit(solution)/shard_map/dot_general | solution.py:75
  (25 shorter events, 0.2 us)
Async XLA Ops:
  0.6 51.2 %copy-start = (bf16[256,1280]{1,0:T(8,128)(2,1)S(1)}, bf16[256,1280]{1,0:T(8,128)(2,1)}, u32[]{:S(2)}) copy-start(bf16[256,1280]{1,0:T(8,128)(2,1)} %param.16) | copy-start | bytes 1966084
  0.6 1.1 %copy-start.1 = (bf16[8,8,1280]{2,1,0:T(8,128)(2,1)S(1)}, bf16[8,8,1280]{2,1,0:T(8,128)(2,1)}, u32[]{:S(2)}) copy-start(bf16[8,8,1280]{2,1,0:T(8,128)(2,1)} %param.10) | copy-start | bytes 491524
  1.8 0.7 %copy-start.7 = (f32[1280]{0:T(1024)S(1)}, f32[1280]{0:T(1024)}, u32[]{:S(2)}) copy-start(f32[1280]{0:T(1024)} %param.11) | copy-start | bytes 15364
  2.0 0.7 %copy-start.6 = (f32[1280]{0:T(1024)S(1)}, f32[1280]{0:T(1024)}, u32[]{:S(2)}) copy-start(f32[1280]{0:T(1024)} %param.12) | copy-start | bytes 15364
  2.8 9.5 %copy-start.3 = (bf16[1280,128]{1,0:T(8,128)(2,1)S(1)}, bf16[1280,128]{1,0:T(8,128)(2,1)}, u32[]{:S(2)}) copy-start(bf16[1280,128]{1,0:T(8,128)(2,1)} %param.14) | copy-start | bytes 983044
  12.3 0.9 %copy-start.8 = (bf16[1280,64]{0,1:T(8,128)(2,1)S(1)}, bf16[1280,64]{0,1:T(8,128)(2,1)}, u32[]{:S(2)}) copy-start(bf16[1280,64]{0,1:T(8,128)(2,1)} %param.13) | copy-start | bytes 491524
  13.6 0.7 %copy-start.2 = (bf16[8,32,192]{2,1,0:T(8,128)(2,1)}, bf16[8,32,192]{2,1,0:T(8,128)(2,1)S(1)}, u32[]{:S(2)}) copy-start(bf16[8,32,192]{2,1,0:T(8,128)(2,1)S(1)} %convolution_convert_fusion) | copy-start | bytes 294916
  14.3 0.8 %copy-start.4 = (bf16[8,32,1,128]{3,1,2,0:T(8,128)(2,1)S(1)}, bf16[8,32,1,128]{3,1,2,0:T(8,128)(2,1)}, u32[]{:S(2)}) copy-start(bf16[8,32,1,128]{3,1,2,0:T(8,128)(2,1)} %param.15) | copy-start | bytes 196612
  15.2 14.3 %slice-start = ((bf16[8,32,192]{2,1,0:T(8,128)(2,1)}), bf16[8,32,64]{2,1,0:T(8,128)(2,1)S(1)}, s32[]{:S(2)}) async-start(bf16[8,32,192]{2,1,0:T(8,128)(2,1)} %copy-done.2), calls=%async_computation.1 | async-start | bytes 131072 | tf_op jit(solution)/shard_map/slice | solution.py:46
  51.7 0.7 %copy-start.5 = (f32[1280]{0:T(1024)S(1)}, f32[1280]{0:T(1024)}, u32[]{:S(2)}) copy-start(f32[1280]{0:T(1024)} %param.17) | copy-start | bytes 15364
where the time goes:
time: 53.9 us; the launch traced here: 53.3 us
  blocking collectives  30.1 us (56%)
  loops' own time  10.6 us (20%)
  local copies, waits for them, and re-layouts  6.62 us (12%)
  matrix products  3.3 us (6%)
  other arithmetic  1.97 us (4%)
  between operations  0.77 us (1%)
    all_gather x1, blocking collectives, shards(): received = lax.all_gather(stale_keyval, 'rows', axis=0, tiled=True)  14.3 us
    another operation x1, loops' own time, shards(): lax.scan(step_band, initial, jnp.arange(band_count, dtype=jnp.int32))  10.6 us
    all_gather x1, blocking collectives, shards(): lax.all_gather(normed, 'cols', axis=1, tiled=True)  9.49 us
    all_to_all x1, blocking collectives, shards(): lax.all_to_all(attention, 'cols', split_axis=1, concat_axis=2, tiled=True)  6.3 us
    unnamed x22, local copies, waits for them, and re-layouts  3.99 us
    dynamic_slice x4, local copies, waits for them, and re-layouts, shards(): lax.scan(step_band, initial, jnp.arange(band_count, dtype=jnp.int32))  2.34 us
    dot_general x4, matrix products, absorb(): jnp.dot(probability.astype(jnp.bfloat16), key_block[:, head_size:], prefe...  1.16 us
    reduce_sum x1, other arithmetic, layer_norm(): row_mean = jnp.mean(values, axis=-1, keepdims=True)  1.1 us

commit v1 on v0

--- a/solution.py
+++ b/solution.py
@@ -69,7 +69,26 @@
         .astype(jnp.bfloat16)
         .reshape(band_rows, full_cols, 1, head_size)
     )
-    values = lax.all_to_all(attention, "cols", split_axis=1, concat_axis=2, tiled=True)
+
+    def point_ratios(inner_x, link_axis):
+        kept_arr = lax.psum(1, link_axis)
+        local_next = lax.axis_index(link_axis)
+        vec_out, spare = (kept_arr, local_next)
+        u_next = inner_x.shape[1] // vec_out
+        state_now = jnp.roll(inner_x, -spare * u_next, 1)
+        value_now = lax.slice_in_dim(state_now, 0, u_next, axis=1)
+        inbox = [value_now]
+        for dd in [*range(1, vec_out)]:
+            u1 = lax.slice_in_dim(state_now, dd * u_next, (dd + 1) * u_next, axis=1)
+            inbox.append(
+                lax.ppermute(
+                    u1, link_axis, [(hop_no, (hop_no + dd) % vec_out) for hop_no in range(vec_out)]
+                )
+            )
+        y_new = jnp.roll(jnp.concatenate(inbox[::-1], axis=2), (spare + 1) * inbox[0].shape[2], 2)
+        return y_new
+
+    values = point_ratios(attention, "cols")
     row_count = values.shape[0]
     flat_values = values.reshape(row_count * values.shape[1], values.shape[2] * values.shape[3])
     result = jnp.dot(flat_values, w_out, preferred_element_type=jnp.float32)

time: 53.9 us -> 51.8 us (0.961)
  blocking collectives: 30.1 us -> 23.7 us
  waiting for transfers between devices: 0 us -> 3 us
  starting transfers between devices: 0 us -> 1.36 us
    all_to_all x1 -> x0, blocking collectives: 6.3 us -> none  [shards(): lax.all_to_all(attention, 'cols', split_axis=1, concat_axis=2, tiled=True)]
    ppermute x0 -> x3, waiting for transfers between devices: none -> 3 us  [point_ratios(): lax.ppermute(u1, link_axis, [(hop_no, (hop_no + dd) % vec_out) for hop_no...]
    ppermute x0 -> x3, starting transfers between devices: none -> 1.36 us  [point_ratios(): lax.ppermute(u1, link_axis, [(hop_no, (hop_no + dd) % vec_out) for hop_no...]
    unnamed x22 -> x27, local copies, waits for them, and re-layouts: 3.99 us -> 3.82 us
  transfers between devices with their start and end apart: 0 -> 3, of which waited for: 0 -> 3; matrix products, arithmetic and copies ran while one was open for 0% -> 0% of each run, Pallas kernels for 0% -> 0%
where the time goes in v1:
time: 51.8 us; the launch traced here: 51.3 us
  blocking collectives  23.7 us (46%)
  loops' own time  10.6 us (20%)
  local copies, waits for them, and re-layouts  6.47 us (12%)
  matrix products  3.29 us (6%)
  waiting for transfers between devices  3 us (6%)
  other arithmetic  2.05 us (4%)
  starting transfers between devices  1.36 us (3%)
  between operations  0.82 us (2%)
    all_gather x1, blocking collectives, shards(): received = lax.all_gather(stale_keyval, 'rows', axis=0, tiled=True)  14.2 us
    another operation x1, loops' own time, shards(): lax.scan(step_band, initial, jnp.arange(band_count, dtype=jnp.int32))  10.6 us
    all_gather x1, blocking collectives, shards(): lax.all_gather(normed, 'cols', axis=1, tiled=True)  9.49 us
    unnamed x27, local copies, waits for them, and re-layouts  3.82 us
    ppermute x3, waiting for transfers between devices, point_ratios(): lax.ppermute(u1, link_axis, [(hop_no, (hop_no + dd) % vec_out) for hop_no...  3 us
    dynamic_slice x4, local copies, waits for them, and re-layouts, shards(): lax.scan(step_band, initial, jnp.arange(band_count, dtype=jnp.int32))  2.34 us
    ppermute x3, starting transfers between devices, point_ratios(): lax.ppermute(u1, link_axis, [(hop_no, (hop_no + dd) % vec_out) for hop_no...  1.36 us
    dot_general x4, matrix products, absorb(): jnp.dot(probability.astype(jnp.bfloat16), key_block[:, head_size:], prefe...  1.16 us
  transfers between devices with their start and end apart: 3, of which 3 were waited for; matrix products, arithmetic and copies ran while one was open for 0% of the time, Pallas kernels for 0%

profile of v1, /device:TPU:0, one launch (start us, length us, event | category | flops | bytes accessed | tf_op | source)
XLA Modules:
  0.0 51.3 jit_solution(16025588693416389132)
XLA Ops:
  0.6 0.0 copy-start
  0.6 0.0 copy-start.1
  0.7 1.1 %convert_reduce_fusion = f32[8,8]{1,0:T(8,128)S(1)} fusion(bf16[8,8,1280]{2,1,0:T(8,128)(2,1)} %param.10), kind=kLoop, calls=%fused_computation.24 | loop fusion | flops 163776 | bytes 164096 | tf_op jit(solution)/shard_map/reduce_sum | solution.py:10
  1.8 0.0 copy-done.1
  1.8 0.0 copy-start.7
  1.8 0.2 fusion.15
  2.0 0.0 copy-start.6
  2.0 0.5 copy-done.7
  2.5 0.2 copy-done.6
  2.7 0.1 fusion.18
  2.9 0.0 copy-start.3
  2.9 9.5 %all_gather.7 = bf16[8,32,1280]{2,1,0:T(8,128)(2,1)S(1)} all-gather(bf16[8,8,1280]{2,1,0:T(8,128)(2,1)S(1)} %fusion.18), channel_id=1, replica_groups=mesh['groups'=2,'rows'=4,'cols'=4] {'cols'}, dimensions={1}, use_global_device_ids=true | all-gather | bytes 819200 | tf_op jit(solution)/shard_map/all_gather | solution.py:41
  12.4 0.0 copy-done.3
  12.4 0.0 copy-start.8
  12.4 0.2 copy.18
  12.5 0.7 %copy-done.8 = bf16[1280,64]{0,1:T(8,128)(2,1)S(1)} copy-done((bf16[1280,64]{0,1:T(8,128)(2,1)S(1)}, bf16[1280,64]{0,1:T(8,128)(2,1)}, u32[]{:S(2)}) %copy-start.8) | copy-done | bytes 163864
  13.3 0.3 convolution_convert_fusion
  13.6 0.0 copy-start.2
  13.6 0.7 %slice_bitcast_fusion = (bf16[8,32,1,128]{3,1,2,0:T(8,128)(2,1)}, bf16[8,32,128]{2,1,0:T(8,128)(2,1)S(1)}) fusion(bf16[8,32,192]{2,1,0:T(8,128)(2,1)S(1)} %convolution_convert_fusion), kind=kLoop, calls=%fused_computation.47 | loop fusion | bytes 196608
  14.4 0.0 copy-done.2
  14.4 0.0 copy-start.4
  14.4 0.8 %copy-done.4 = bf16[8,32,1,128]{3,1,2,0:T(8,128)(2,1)S(1)} copy-done((bf16[8,32,1,128]{3,1,2,0:T(8,128)(2,1)S(1)}, bf16[8,32,1,128]{3,1,2,0:T(8,128)(2,1)}, u32[]{:S(2)}) %copy-start.4) | copy-done | bytes 65560
  15.2 0.0 slice-start
  15.2 14.2 %all_gather.6 = bf16[32,32,1,128]{3,1,2,0:T(8,128)(2,1)S(1)} all-gather(bf16[8,32,1,128]{3,1,2,0:T(8,128)(2,1)S(1)} %copy-done.4), channel_id=1, replica_groups=mesh['groups'=2,'rows'=4,'cols'=4] {'rows'}, dimensions={0}, use_global_device_ids=true | all-gather | bytes 327680 | tf_op jit(solution)/shard_map/all_gather | solution.py:57
  29.4 0.0 slice-done
  29.4 15.4 %while.15 = (s32[]{:T(128)}, f32[256]{0:T(256)S(1)}, f32[256]{0:T(256)S(1)}, f32[256,64]{0,1:T(8,128)S(1)}, s32[4]{0:T(128)S(1)}, /*index=5*/s32[]{:T(128)}, bf1...) while((s32[]{:T(128)}, f32[256]{0:T(256)S(1)}, ...), condition=%wide.region_5.6_spmd.clone, body=%wide.region_2.5_spmd.clone.sunk | while | flops 17253640 | bytes 1294525 | solution.py:65
  29.4 0.6 %dynamic_slice.32 = s32[1]{0:T(128)} dynamic-slice(s32[4]{0:T(128)S(1)} %get-tuple-element.206, s32[]{:T(128)} %get-tuple-element.190), dynamic_slice_sizes={1} | dynamic-slice | bytes 12 | tf_op jit(solution)/shard_map/while/body/jit(dynamic_index_in_dim)/dynamic_slice | solution.py:65
  32.6 0.2 fusion.36
  32.9 0.1 fusion.38
  32.9 0.3 convolution_add_fusion.3
  33.3 0.6 %dynamic_slice.32 = s32[1]{0:T(128)} dynamic-slice(s32[4]{0:T(128)S(1)} %get-tuple-element.206, s32[]{:T(128)} %get-tuple-element.190), dynamic_slice_sizes={1} | dynamic-slice | bytes 12 | tf_op jit(solution)/shard_map/while/body/jit(dynamic_index_in_dim)/dynamic_slice | solution.py:65
  36.5 0.2 fusion.36
  36.7 0.1 fusion.38
  36.8 0.3 convolution_add_fusion.3
  37.1 0.6 %dynamic_slice.32 = s32[1]{0:T(128)} dynamic-slice(s32[4]{0:T(128)S(1)} %get-tuple-element.206, s32[]{:T(128)} %get-tuple-element.190), dynamic_slice_sizes={1} | dynamic-slice | bytes 12 | tf_op jit(solution)/shard_map/while/body/jit(dynamic_index_in_dim)/dynamic_slice | solution.py:65
  40.3 0.2 fusion.36
  40.6 0.1 fusion.38
  40.6 0.3 convolution_add_fusion.3
  41.0 0.6 %dynamic_slice.32 = s32[1]{0:T(128)} dynamic-slice(s32[4]{0:T(128)S(1)} %get-tuple-element.206, s32[]{:T(128)} %get-tuple-element.190), dynamic_slice_sizes={1} | dynamic-slice | bytes 12 | tf_op jit(solution)/shard_map/while/body/jit(dynamic_index_in_dim)/dynamic_slice | solution.py:65
  44.2 0.2 fusion.36
  44.4 0.1 fusion.38
  44.5 0.3 convolution_add_fusion.3
  44.8 0.1 copy.19
  44.9 0.1 divide_convert_fusion
  45.0 0.1 fusion.19
  45.1 0.1 collective-permute-start
  45.2 1.2 %collective-permute-start.1 = (bf16[8,8,1,64]{3,1,0,2:T(8,128)(2,1)S(1)}, bf16[8,8,1,64]{3,1,0,2:T(8,128)(2,1)S(1)}, u32[]{:S(2)}, u32[]{:S(2)}) collective-permute-start(bf16[8,8,1,64]{3,1,0,2:T(8,128)(2,1)S(1)} %get-tuple-element.113), channel_id=1, source_target_pairs={{0,2},{1,3},{2,0},{3,1},{4,6},{5,7},{6,4},{7,5},{8,10},{9,11},{10,... | collective-permute-start | bytes 24584 | tf_op jit(solution)/shard_map/ppermute | solution.py:84
  46.3 0.2 collective-permute-start.2
  46.5 0.1 collective-permute-done
  46.6 2.4 %collective-permute-done.1 = bf16[8,8,1,64]{3,1,0,2:T(8,128)(2,1)S(1)} collective-permute-done((bf16[8,8,1,64]{3,1,0,2:T(8,128)(2,1)S(1)}, bf16[8,8,1,64]{3,1,0,2:T(8,128)(2,1)S(1)}, u32[]{:S(2)}, u32[]{:S(2)}) %collective-permute-start.1) | collective-permute-done | bytes 8224 | tf_op jit(solution)/shard_map/ppermute | solution.py:84
  49.0 0.5 collective-permute-done.2
  49.6 0.1 copy.20
  49.6 0.0 copy-start.5
  49.7 0.1 dot_general.15
  49.8 0.0 copy-done
  49.8 0.6 %copy-done.5 = f32[1280]{0:T(1024)S(1)} copy-done((f32[1280]{0:T(1024)S(1)}, f32[1280]{0:T(1024)}, u32[]{:S(2)}) %copy-start.5) | copy-done | bytes 5144
  50.3 0.9 %fusion.9 = bf16[8,8,1280]{2,1,0:T(8,128)(2,1)} fusion(bf16[8,8,256]{2,1,0:T(8,128)(2,1)S(1)} %dot_general.15, bf16[256,1280]{1,0:T(8,128)(2,1)S(1)} %copy-done, bf16[8,8,1280]{2,1,0:T(8,128)(2,1)S(1)} %copy-done.1, f32[1280]{0:T(1024)S(1)} %copy-done.5), kind=kOutput, calls=%fused_computation.17 | convolution fusion | flops 42270720 | bytes 1020928 | tf_op jit(solution)/shard_map/dot_general | solution.py:94
  (32 shorter events, 0.3 us)
Async XLA Ops:
  0.6 49.1 %copy-start = (bf16[256,1280]{1,0:T(8,128)(2,1)S(1)}, bf16[256,1280]{1,0:T(8,128)(2,1)}, u32[]{:S(2)}) copy-start(bf16[256,1280]{1,0:T(8,128)(2,1)} %param.16) | copy-start | bytes 1966084
  0.6 1.2 %copy-start.1 = (bf16[8,8,1280]{2,1,0:T(8,128)(2,1)S(1)}, bf16[8,8,1280]{2,1,0:T(8,128)(2,1)}, u32[]{:S(2)}) copy-start(bf16[8,8,1280]{2,1,0:T(8,128)(2,1)} %param.10) | copy-start | bytes 491524
  1.8 0.7 %copy-start.7 = (f32[1280]{0:T(1024)S(1)}, f32[1280]{0:T(1024)}, u32[]{:S(2)}) copy-start(f32[1280]{0:T(1024)} %param.11) | copy-start | bytes 15364
  2.0 0.7 %copy-start.6 = (f32[1280]{0:T(1024)S(1)}, f32[1280]{0:T(1024)}, u32[]{:S(2)}) copy-start(f32[1280]{0:T(1024)} %param.12) | copy-start | bytes 15364
  2.9 9.5 %copy-start.3 = (bf16[1280,128]{1,0:T(8,128)(2,1)S(1)}, bf16[1280,128]{1,0:T(8,128)(2,1)}, u32[]{:S(2)}) copy-start(bf16[1280,128]{1,0:T(8,128)(2,1)} %param.14) | copy-start | bytes 983044
  12.4 0.9 %copy-start.8 = (bf16[1280,64]{0,1:T(8,128)(2,1)S(1)}, bf16[1280,64]{0,1:T(8,128)(2,1)}, u32[]{:S(2)}) copy-start(bf16[1280,64]{0,1:T(8,128)(2,1)} %param.13) | copy-start | bytes 491524
  13.6 0.7 %copy-start.2 = (bf16[8,32,192]{2,1,0:T(8,128)(2,1)}, bf16[8,32,192]{2,1,0:T(8,128)(2,1)S(1)}, u32[]{:S(2)}) copy-start(bf16[8,32,192]{2,1,0:T(8,128)(2,1)S(1)} %convolution_convert_fusion) | copy-start | bytes 294916
  14.4 0.8 %copy-start.4 = (bf16[8,32,1,128]{3,1,2,0:T(8,128)(2,1)S(1)}, bf16[8,32,1,128]{3,1,2,0:T(8,128)(2,1)}, u32[]{:S(2)}) copy-start(bf16[8,32,1,128]{3,1,2,0:T(8,128)(2,1)} %param.15) | copy-start | bytes 196612
  15.2 14.2 %slice-start = ((bf16[8,32,192]{2,1,0:T(8,128)(2,1)}), bf16[8,32,64]{2,1,0:T(8,128)(2,1)S(1)}, s32[]{:S(2)}) async-start(bf16[8,32,192]{2,1,0:T(8,128)(2,1)} %copy-done.2), calls=%async_computation | async-start | bytes 131072 | tf_op jit(solution)/shard_map/slice | solution.py:46
  45.1 1.5 %collective-permute-start = (bf16[8,8,1,64]{3,1,0,2:T(8,128)(2,1)S(1)}, bf16[8,8,1,64]{3,1,0,2:T(8,128)(2,1)S(1)}, u32[]{:S(2)}, u32[]{:S(2)}) collective-permute-start(bf16[8,8,1,64]{3,1,0,2:T(8,128)(2,1)S(1)} %get-tuple-element.114), channel_id=1, source_target_pairs={{0,3},{1,0},{2,1},{3,2},{4,7},{5,4},{6,5},{7,6},{8,11},{9,8},{10,9... | collective-permute-start | bytes 24584 | tf_op jit(solution)/shard_map/ppermute | solution.py:84
  45.2 3.8 %collective-permute-start.1 = (bf16[8,8,1,64]{3,1,0,2:T(8,128)(2,1)S(1)}, bf16[8,8,1,64]{3,1,0,2:T(8,128)(2,1)S(1)}, u32[]{:S(2)}, u32[]{:S(2)}) collective-permute-start(bf16[8,8,1,64]{3,1,0,2:T(8,128)(2,1)S(1)} %get-tuple-element.113), channel_id=1, source_target_pairs={{0,2},{1,3},{2,0},{3,1},{4,6},{5,7},{6,4},{7,5},{8,10},{9,11},{10,... | collective-permute-start | bytes 24584 | tf_op jit(solution)/shard_map/ppermute | solution.py:84
  46.3 3.2 %collective-permute-start.2 = (bf16[8,8,1,64]{3,1,0,2:T(8,128)(2,1)S(1)}, bf16[8,8,1,64]{3,1,0,2:T(8,128)(2,1)S(1)}, u32[]{:S(2)}, u32[]{:S(2)}) collective-permute-start(bf16[8,8,1,64]{3,1,0,2:T(8,128)(2,1)S(1)} %get-tuple-element.112), channel_id=1, source_target_pairs={{0,1},{1,2},{2,3},{3,0},{4,5},{5,6},{6,7},{7,4},{8,9},{9,10},{10,1... | collective-permute-start | bytes 24584 | tf_op jit(solution)/shard_map/ppermute | solution.py:84
  49.6 0.7 %copy-start.5 = (f32[1280]{0:T(1024)S(1)}, f32[1280]{0:T(1024)}, u32[]{:S(2)}) copy-start(f32[1280]{0:T(1024)} %param.17) | copy-start | bytes 15364
